TPU v7x, 512 devices: a whole 4x4x16 slice. The times are simulated.
512 devices in a mesh: expert: 64 (over x, z), dp: 4 (over y), test: 2 (over core).
Axes of the slice: x: 4, y: 4, z: 16, core: 2. Of those that a mesh axis runs over, the one named last changes fastest.
Arguments:
- tokens: bfloat16 [16384, 3584], P(('expert', 'dp'), 'test'), may hold values from -6 to 6
- out_grad: bfloat16 [16384, 3584], P(('expert', 'dp'), 'test'), may hold values from -6 to 6
- route_ids: int32 [16384, 8], P(('expert', 'dp')), may hold values from 0 to 255, as said below
- route_slots: int32 [16384, 8], P(('expert', 'dp')), may hold values from -1 to 1, as said below
- route_weight: bfloat16 [16384, 8], P(('expert', 'dp')), may hold values from 0.19921875 to 1
- w_gate: bfloat16 [64, 3584, 1024], P('expert', None, ('dp', 'test')), may hold values from -0.09375 to 0.09375
- w_up: bfloat16 [64, 3584, 1024], P('expert', None, ('dp', 'test')), may hold values from -0.09375 to 0.09375
- w_down: bfloat16 [64, 1024, 3584], P('expert', ('dp', 'test')), may hold values from -0.1875 to 0.1875
- proj_hidden: bfloat16 [64, 64, 1024], P('expert', None, ('dp', 'test')), may hold values from -0.1875 to 0.1875
- proj_grad: bfloat16 [64, 64, 3584], P('expert'), may hold values from -0.09375 to 0.09375
- test_feats: bfloat16 [64, 256, 4096], P('expert', 'test'), may hold values from -0.09375 to 0.09375
Outputs:
- in_grad: bfloat16 [16384, 3584], P(('expert', 'dp'), 'test')
- scores: float32 [16384, 256], P(('expert', 'dp'), 'test')
Inputs may be any that keep to these rules, and one draw needn't show every extreme that they name: `route_ids`: each row names 8 different experts. `route_slots`: A route's slot is -1 exactly when its expert is 64 or more, or when 2 earlier tokens of the same aligned block of 64 rows already take that expert; otherwise it is the number of earlier tokens of that block routed to that expert.
All inputs are finite; a program needn't handle non-finite values.
Results may differ from a plain program's by a relative error of at most 0.0065.
Values may be sent and summed in bfloat16 or wider, within the bound.
A program may use at most 64 MiB of HBM per device.

v0:
```python
import jax
import jax.numpy as jnp
from jax import lax
from jax.sharding import PartitionSpec as P

CAP = 2


def pick_tables(ids_in, slots_in, weights_in, experts):
    live_mask = (slots_in >= 0) & (ids_in < experts)
    slot_code = jnp.where(live_mask, ids_in * CAP + slots_in, -1)
    columns = jnp.arange(experts * CAP, dtype=jnp.int32)
    matches = slot_code[:, :, None] == columns[None, None, :]
    picks = jnp.sum(matches.astype(jnp.float32), axis=1)
    weighted = jnp.sum(jnp.where(matches, weights_in.astype(jnp.float32)[:, :, None], 0.0), axis=1)
    return (picks, weighted)


def expert_pass(flat_in, flat_grad, gate_w, up_w, down_w, hid_proj):
    gate_pre = jnp.dot(flat_in, gate_w, preferred_element_type=jnp.float32)
    up_pre = jnp.dot(flat_in, up_w, preferred_element_type=jnp.float32)
    sigmoid_gate = jax.nn.sigmoid(gate_pre)
    act_gate = gate_pre * sigmoid_gate
    hidden = (act_gate * up_pre).astype(jnp.bfloat16)
    proj_part = lax.dot_general(
        hidden, hid_proj, (((1,), (1,)), ((), ())), preferred_element_type=jnp.float32
    )
    hid_grad = lax.dot_general(
        flat_grad, down_w, (((1,), (1,)), ((), ())), preferred_element_type=jnp.float32
    )
    up_grad = (hid_grad * act_gate).astype(jnp.bfloat16)
    gate_grad = (hid_grad * up_pre * sigmoid_gate * (1.0 + gate_pre * (1.0 - sigmoid_gate))).astype(
        jnp.bfloat16
    )
    return (proj_part, gate_grad, up_grad)


def score_rows(hidden_vec, grad_vec, test_rows):
    row_total = hidden_vec.shape[0]
    feature = (
        (hidden_vec[:, :, None] * grad_vec[:, None, :]).reshape(row_total, -1).astype(jnp.bfloat16)
    )
    return lax.dot_general(
        feature, test_rows, (((1,), (1,)), ((), ())), preferred_element_type=jnp.float32
    )


def on_device(
    tokens,
    out_grad,
    route_ids,
    route_slots,
    route_weight,
    w_gate,
    w_up,
    w_down,
    proj_hidden,
    proj_grad,
    test_feats,
):
    experts = lax.axis_size("expert")
    groups = lax.axis_size("dp")
    halves = lax.axis_size("test")
    tok_rows = tokens.shape[0]
    half_width = tokens.shape[1]
    slots_all = experts * CAP
    full_in, full_grad = (
        lax.all_gather(tokens, "test", axis=1, tiled=True),
        lax.all_gather(out_grad, "test", axis=1, tiled=True),
    )
    full_width = full_in.shape[1]
    grad_proj = proj_grad[0]
    test_rows = test_feats[0]
    own_pick, own_weight = pick_tables(route_ids, route_slots, route_weight, experts)
    all_in, all_grad, all_ids, all_slots, all_weight = (
        lax.all_gather(full_in, "dp", axis=0, tiled=True),
        lax.all_gather(full_grad, "dp", axis=0, tiled=True),
        lax.all_gather(route_ids, "dp", axis=0, tiled=True),
        lax.all_gather(route_slots, "dp", axis=0, tiled=True),
        lax.all_gather(route_weight, "dp", axis=0, tiled=True),
    )
    group_tok = all_in.shape[0]
    pick_all, weight_all = pick_tables(all_ids, all_slots, all_weight, experts)
    owner_idx = jnp.arange(group_tok, dtype=jnp.int32) // tok_rows
    in_group = (owner_idx[None, :] == jnp.arange(groups, dtype=jnp.int32)[:, None]).astype(
        jnp.float32
    )
    select = (
        (pick_all.T.reshape(experts, 1, CAP, group_tok) * in_group.reshape(1, groups, 1, group_tok))
        .reshape(-1, group_tok)
        .astype(jnp.bfloat16)
    )
    select_w = (
        (
            weight_all.T.reshape(experts, 1, CAP, group_tok)
            * in_group.reshape(1, groups, 1, group_tok)
        )
        .reshape(-1, group_tok)
        .astype(jnp.bfloat16)
    )
    in_buf = jnp.dot(select, all_in, preferred_element_type=jnp.float32).astype(jnp.bfloat16)
    grad_buf = jnp.dot(select_w, all_grad, preferred_element_type=jnp.float32).astype(jnp.bfloat16)
    rows_per = groups * CAP
    recv_in, recv_grad = (
        lax.all_to_all(
            in_buf.reshape(experts, rows_per, full_width),
            "expert",
            split_axis=0,
            concat_axis=0,
            tiled=True,
        ),
        lax.all_to_all(
            grad_buf.reshape(experts, rows_per, full_width),
            "expert",
            split_axis=0,
            concat_axis=0,
            tiled=True,
        ),
    )
    flat_in = recv_in.reshape(-1, full_width)
    flat_grad = recv_grad.reshape(-1, full_width)
    gate_w = w_gate[0]
    up_w = w_up[0]
    proj_part, gate_grad, up_grad = expert_pass(
        flat_in, flat_grad, gate_w, up_w, w_down[0], proj_hidden[0]
    )
    parts = lax.dot_general(
        gate_grad, gate_w, (((1,), (1,)), ((), ())), preferred_element_type=jnp.float32
    )
    parts = (
        parts
        + lax.dot_general(
            up_grad, up_w, (((1,), (1,)), ((), ())), preferred_element_type=jnp.float32
        )
    ).astype(jnp.bfloat16)
    hidden_vec = lax.psum(proj_part, ("dp", "test"))
    my_group = lax.axis_index("dp")
    hid_mine = lax.dynamic_index_in_dim(
        hidden_vec.reshape(experts, groups, CAP, -1), my_group, 1, keepdims=False
    ).reshape(slots_all, -1)
    grad_rows = lax.dynamic_index_in_dim(
        recv_grad.reshape(experts, groups, CAP, full_width), my_group, 1, keepdims=False
    ).reshape(slots_all, full_width)
    grad_mine = lax.dot_general(
        grad_rows, grad_proj, (((1,), (1,)), ((), ())), preferred_element_type=jnp.float32
    )
    route_score = (
        score_rows(hid_mine, grad_mine, test_rows).astype(jnp.bfloat16).reshape(experts, CAP, -1)
    )
    back_parts, back_score = (
        lax.all_to_all(
            parts.reshape(experts, rows_per, full_width),
            "expert",
            split_axis=0,
            concat_axis=0,
            tiled=True,
        ),
        lax.all_to_all(route_score, "expert", split_axis=0, concat_axis=0, tiled=True),
    )
    part_rows = back_parts.reshape(-1, full_width)
    first_row = jnp.int32(0)
    pieces = []
    for block_step in range(tok_rows * lax.axis_size(("dp", "test")) // tok_rows):
        block_idx = first_row // tok_rows + block_step
        owner_block = block_idx // halves
        half_idx = block_idx % halves
        picked_cols = lax.dynamic_slice_in_dim(select, owner_block * tok_rows, tok_rows, 1)
        part_cols = lax.dynamic_slice_in_dim(part_rows, half_idx * half_width, half_width, 1)
        pieces.append(
            lax.dot_general(
                picked_cols, part_cols, (((0,), (0,)), ((), ())), preferred_element_type=jnp.float32
            )
        )
    in_grad = lax.psum_scatter(
        jnp.concatenate(pieces, axis=0), ("dp", "test"), scatter_dimension=0, tiled=True
    ).astype(jnp.bfloat16)
    scores_out = jnp.dot(
        own_pick.astype(jnp.bfloat16),
        back_score.reshape(slots_all, -1),
        preferred_element_type=jnp.float32,
    )
    return (in_grad, scores_out)


def solution(mesh):
    placed = (
        P(("expert", "dp"), "test"),
        P(("expert", "dp"), "test"),
        P(("expert", "dp"), None),
        P(("expert", "dp"), None),
        P(("expert", "dp"), None),
        P("expert", None, ("dp", "test")),
        P("expert", None, ("dp", "test")),
        P("expert", ("dp", "test"), None),
        P("expert", None, ("dp", "test")),
        P("expert", None, None),
        P("expert", "test", None),
    )
    return jax.shard_map(
        on_device,
        mesh=mesh,
        in_specs=placed,
        out_specs=(P(("expert", "dp"), "test"), P(("expert", "dp"), "test")),
        check_vma=False,
    )
```

profile of v0, /device:TPU:1, one launch (start us, length us, event | category | flops | bytes accessed | tf_op | source)
XLA Modules:
  0.0 657.6 jit_solution(9366702021190305749)
XLA Ops:
  7.2 10.6 %all_gather.26 = bf16[64,3584]{1,0:T(8,128)(2,1)} all-gather(bf16[64,1792]{1,0:T(8,128)(2,1)} %param.11), channel_id=1, replica_groups=mesh['expert'=64,'dp'=4,'test'=2] {'test'}, dimensions={1}, use_global_device_ids=true | all-gather | bytes 688128 | tf_op jit(solution)/shard_map/all_gather | solution.py:68
  17.8 9.3 %all-gather = s32[4,64,8]{1,2,0:T(8,128)S(1)} all-gather(s32[1,64,8]{1,2,0:T(8,128)} %bitcast.65), channel_id=1, replica_groups=mesh['expert'=64,'dp'=4,'test'=2] {'dp'}, dimensions={0}, use_global_device_ids=true | all-gather | bytes 10240 | tf_op jit(solution)/shard_map/all_gather | solution.py:79
  27.1 9.3 %all-gather.1 = s32[4,64,8]{1,2,0:T(8,128)S(1)} all-gather(s32[1,64,8]{1,2,0:T(8,128)} %bitcast.66), channel_id=1, replica_groups=mesh['expert'=64,'dp'=4,'test'=2] {'dp'}, dimensions={0}, use_global_device_ids=true | all-gather | bytes 10240 | tf_op jit(solution)/shard_map/all_gather | solution.py:78
  36.5 9.6 %all-gather.2 = bf16[4,64,8]{1,2,0:T(8,128)(2,1)S(1)} all-gather(bf16[1,64,8]{1,2,0:T(8,128)(2,1)} %bitcast.67), channel_id=1, replica_groups=mesh['expert'=64,'dp'=4,'test'=2] {'dp'}, dimensions={0}, use_global_device_ids=true | all-gather | bytes 5120 | tf_op jit(solution)/shard_map/all_gather | solution.py:80
  48.6 4.3 all-gather.8.cloned.1.call-done
  52.9 4.4 fusion.1
  57.3 15.7 %all-to-all-start.1 = ((bf16[64,8,3584]{2,1,0:T(8,128)(2,1)}), bf16[64,8,3584]{2,1,0:T(8,128)(2,1)}, u32[]{:S(2)}, u32[]{:S(2)}) async-start(bf16[64,8,3584]{2,1,0:T(8,128)(2,1)} %fusion.1), calls=%async_computation.1 | async-start | bytes 7340032 | tf_op jit(solution)/shard_map/all_to_all | solution.py:105
  73.1 3.2 all_gather.24
  76.4 36.7 %all-gather.6.cloned.1.call-done = bf16[256,3584]{1,0:T(8,128)(2,1)} async-done(((bf16[64,3584]{1,0:T(8,128)(2,1)}), bf16[256,3584]{1,0:T(8,128)(2,1)}) %all-gather.6.cloned.1.call-update) | async-done | bytes 1835024 | tf_op jit(solution)/shard_map/all_gather | solution.py:77
  113.1 4.5 fusion
  117.6 114.7 %all-to-all-done.1 = bf16[64,8,3584]{2,1,0:T(8,128)(2,1)} async-done(((bf16[64,8,3584]{2,1,0:T(8,128)(2,1)}), bf16[64,8,3584]{2,1,0:T(8,128)(2,1)}, u32[]{:S(2)}, u32[]{:S(2)}) %all-to-all-start.1) | async-done | bytes 3670048 | tf_op jit(solution)/shard_map/all_to_all | solution.py:105
  232.3 13.6 %all-to-all-start = ((bf16[64,8,3584]{2,1,0:T(8,128)(2,1)}), bf16[64,8,3584]{2,1,0:T(8,128)(2,1)}, u32[]{:S(2)}, u32[]{:S(2)}) async-start(bf16[64,8,3584]{2,1,0:T(8,128)(2,1)} %fusion), calls=%async_computation | async-start | bytes 7340032 | tf_op jit(solution)/shard_map/all_to_all | solution.py:112
  245.9 3.2 fusion.3
  249.1 3.8 fusion.5
  253.0 152.1 %all-to-all-done = bf16[64,8,3584]{2,1,0:T(8,128)(2,1)} async-done(((bf16[64,8,3584]{2,1,0:T(8,128)(2,1)}), bf16[64,8,3584]{2,1,0:T(8,128)(2,1)}, u32[]{:S(2)}, u32[]{:S(2)}) %all-to-all-start) | async-done | bytes 3670048 | tf_op jit(solution)/shard_map/all_to_all | solution.py:112
  405.1 3.4 fusion.7
  409.7 3.0 fusion.2
  412.8 13.7 %all-to-all-start.2 = ((bf16[64,8,3584]{2,1,0:T(8,128)(2,1)}), bf16[64,8,3584]{2,1,0:T(8,128)(2,1)}, u32[]{:S(2)}, u32[]{:S(2)}) async-start(bf16[64,8,3584]{2,1,0:T(8,128)(2,1)} %fusion.2), calls=%async_computation.2 | async-start | bytes 7340032 | tf_op jit(solution)/shard_map/all_to_all | solution.py:151
  427.7 158.0 %all-to-all-done.2 = bf16[64,8,3584]{2,1,0:T(8,128)(2,1)} async-done(((bf16[64,8,3584]{2,1,0:T(8,128)(2,1)}), bf16[64,8,3584]{2,1,0:T(8,128)(2,1)}, u32[]{:S(2)}, u32[]{:S(2)}) %all-to-all-start.2) | async-done | bytes 3670048 | tf_op jit(solution)/shard_map/all_to_all | solution.py:151
  591.3 2.8 convolution_dynamic-update-slice_fusion.5
  594.1 2.9 convolution_dynamic-update-slice_fusion.4
  608.1 8.1 %reshape.114 = bf16[64,4,2,3584]{3,2,1,0:T(2,128)(2,1)} reshape(bf16[64,8,3584]{2,1,0:T(8,128)(2,1)} %all-to-all-done) | data formatting | bytes 7340032 | tf_op jit(solution)/shard_map/reshape | solution.py:142
  621.3 13.4 %all-to-all-start.3 = ((bf16[64,2,128]{2,1,0:T(2,128)(2,1)}), bf16[64,2,128]{2,1,0:T(2,128)(2,1)S(1)}, u32[]{:S(2)}, u32[]{:S(2)}) async-start(bf16[64,2,128]{2,1,0:T(2,128)(2,1)} %bitcast.22), calls=%async_computation.4 | async-start | bytes 65536 | tf_op jit(solution)/shard_map/all_to_all | solution.py:158
  634.9 13.0 %all-to-all-done.3 = bf16[64,2,128]{2,1,0:T(2,128)(2,1)S(1)} async-done(((bf16[64,2,128]{2,1,0:T(2,128)(2,1)}), bf16[64,2,128]{2,1,0:T(2,128)(2,1)S(1)}, u32[]{:S(2)}, u32[]{:S(2)}) %all-to-all-start.3) | async-done | bytes 32800 | tf_op jit(solution)/shard_map/all_to_all | solution.py:158
  (63 shorter events, 30.2 us)
Async XLA Ops:
  7.2 613.0 %copy-start = (bf16[1,128,4096]{2,1,0:T(8,128)(2,1)S(1)}, bf16[1,128,4096]{2,1,0:T(8,128)(2,1)}, u32[]{:S(2)}) copy-start(bf16[1,128,4096]{2,1,0:T(8,128)(2,1)} %param.21) | copy-start | bytes 3145732
  7.2 45.7 %all-gather.8.cloned.1.call-start = ((), (), s32[]{:S(2)}) async-start(), calls=%async_computation.6 | async-start | bytes 2293760 | tf_op jit(solution)/shard_map/all_gather | solution.py:76
  57.3 15.8 %copy-start.6 = (bf16[64,1792]{1,0:T(8,128)(2,1)S(1)}, bf16[64,1792]{1,0:T(8,128)(2,1)}, u32[]{:S(2)}) copy-start(bf16[64,1792]{1,0:T(8,128)(2,1)} %param.12) | copy-start | bytes 688132
  57.3 175.0 %all-to-all-start.1 = ((bf16[64,8,3584]{2,1,0:T(8,128)(2,1)}), bf16[64,8,3584]{2,1,0:T(8,128)(2,1)}, u32[]{:S(2)}, u32[]{:S(2)}) async-start(bf16[64,8,3584]{2,1,0:T(8,128)(2,1)} %fusion.1), calls=%async_computation.1 | async-start | bytes 7340032 | tf_op jit(solution)/shard_map/all_to_all | solution.py:105
  73.0 40.1 %all-gather.6.cloned.1.call-start = ((), (), s32[]{:S(2)}) async-start(), calls=%async_computation.5 | async-start | bytes 2293760 | tf_op jit(solution)/shard_map/all_gather | solution.py:77
  117.6 128.3 %copy-start.1 = (bf16[1,3584,128]{2,1,0:T(8,128)(2,1)S(1)}, bf16[1,3584,128]{2,1,0:T(8,128)(2,1)}, u32[]{:S(2)}) copy-start(bf16[1,3584,128]{2,1,0:T(8,128)(2,1)} %param.16) | copy-start | bytes 2752516
  232.3 172.8 %all-to-all-start = ((bf16[64,8,3584]{2,1,0:T(8,128)(2,1)}), bf16[64,8,3584]{2,1,0:T(8,128)(2,1)}, u32[]{:S(2)}, u32[]{:S(2)}) async-start(bf16[64,8,3584]{2,1,0:T(8,128)(2,1)} %fusion), calls=%async_computation | async-start | bytes 7340032 | tf_op jit(solution)/shard_map/all_to_all | solution.py:112
  245.9 3.2 copy-start.2
  405.1 3.4 copy-start.3
  412.8 13.8 %copy-start.4 = (f32[512,128]{1,0:T(8,128)S(1)}, f32[512,128]{1,0:T(8,128)}, u32[]{:S(2)}) copy-start(f32[512,128]{1,0:T(8,128)} %fusion.5) | copy-start | bytes 786436
  412.8 13.8 %copy-start.9 = (bf16[1,64,128]{2,1,0:T(8,128)(2,1)S(1)}, bf16[1,64,128]{2,1,0:T(8,128)(2,1)}, u32[]{:S(2)}) copy-start(bf16[1,64,128]{2,1,0:T(8,128)(2,1)} %param.19) | copy-start | bytes 49156
  412.8 173.0 %all-to-all-start.2 = ((bf16[64,8,3584]{2,1,0:T(8,128)(2,1)}), bf16[64,8,3584]{2,1,0:T(8,128)(2,1)}, u32[]{:S(2)}, u32[]{:S(2)}) async-start(bf16[64,8,3584]{2,1,0:T(8,128)(2,1)} %fusion.2), calls=%async_computation.2 | async-start | bytes 7340032 | tf_op jit(solution)/shard_map/all_to_all | solution.py:151
  426.5 192.4 %all-reduce.2.cloned.1.call-start = ((), (), s32[]{:S(2)}) async-start(), calls=%async_computation.8 | async-start | bytes 524288 | tf_op jit(solution)/shard_map/psum | solution.py:136
  427.5 221.9 %reduce-scatter.2.cloned.1.call-start = ((), (), s32[]{:S(2)}) async-start(), calls=%async_computation.7 | async-start | bytes 4128768 | tf_op jit(solution)/shard_map/reduce_scatter | solution.py:174
  616.2 2.2 copy-start.5
  618.1 16.5 %copy-start.7 = (s32[64,8]{0,1:T(8,128)S(1)}, s32[64,8]{0,1:T(8,128)}, u32[]{:S(2)}) copy-start(s32[64,8]{0,1:T(8,128)} %param.14) | copy-start | bytes 6148
  618.1 16.5 %copy-start.8 = (s32[64,8]{0,1:T(8,128)S(1)}, s32[64,8]{0,1:T(8,128)}, u32[]{:S(2)}) copy-start(s32[64,8]{0,1:T(8,128)} %param.13) | copy-start | bytes 6148
  621.3 26.6 %all-to-all-start.3 = ((bf16[64,2,128]{2,1,0:T(2,128)(2,1)}), bf16[64,2,128]{2,1,0:T(2,128)(2,1)S(1)}, u32[]{:S(2)}, u32[]{:S(2)}) async-start(bf16[64,2,128]{2,1,0:T(2,128)(2,1)} %bitcast.22), calls=%async_computation.4 | async-start | bytes 65536 | tf_op jit(solution)/shard_map/all_to_all | solution.py:158
Sparse Core Ops, SparseCore 0:
  18.0 34.8 all-gather.7
  76.4 36.6 all-gather.5
  429.6 75.9 all-reduce.1
  608.2 41.0 reduce-scatter.1
where the time goes:
time: 660 us; the launch traced here: 658 us
  waiting for transfers between devices  480 us (73%)
  starting transfers between devices  56.7 us (9%)
  matrix products  49.1 us (7%)
  blocking collectives  41.9 us (6%)
  between operations  14.1 us (2%)
  local copies, waits for them, and re-layouts  12.1 us (2%)
    all_to_all x1, waiting for transfers between devices, on_device(): lax.all_to_all(parts.reshape(experts, rows_per, full_width), 'expert', sp...  158 us
    all_to_all x1, waiting for transfers between devices, on_device(): lax.all_to_all(grad_buf.reshape(experts, rows_per, full_width), 'expert',...  152 us
    all_to_all x1, waiting for transfers between devices, on_device(): lax.all_to_all(in_buf.reshape(experts, rows_per, full_width), 'expert', s...  115 us
    all_gather x1, waiting for transfers between devices, on_device(): lax.all_gather(full_grad, 'dp', axis=0, tiled=True)  36.7 us
    dot_general x8, matrix products, on_device(): lax.dot_general(picked_cols, part_cols, (((0,), (0,)), ((), ())), preferr...  22.3 us
    all_to_all x1, starting transfers between devices, on_device(): lax.all_to_all(in_buf.reshape(experts, rows_per, full_width), 'expert', s...  15.7 us
    all_to_all x1, starting transfers between devices, on_device(): lax.all_to_all(parts.reshape(experts, rows_per, full_width), 'expert', sp...  13.7 us
    all_to_all x1, starting transfers between devices, on_device(): lax.all_to_all(grad_buf.reshape(experts, rows_per, full_width), 'expert',...  13.6 us
  transfers between devices with their start and end apart: 8, of which 7 were waited for; matrix products, arithmetic and copies ran while one was open for 8% of the time, Pallas kernels for 0%

commit v1 on v0

v1 whole, which is shorter than its diff:
```python
import jax
import jax.numpy as jnp
from jax import lax
from jax.sharding import PartitionSpec as P

CAP = 2


def pick_tables(ids_in, slots_in, weights_in, experts):
    live_mask = (slots_in >= 0) & (ids_in < experts)
    slot_code = jnp.where(live_mask, ids_in * CAP + slots_in, -1)
    columns = jnp.arange(experts * CAP, dtype=jnp.int32)
    matches = slot_code[:, :, None] == columns[None, None, :]
    picks = jnp.sum(matches.astype(jnp.float32), axis=1)
    weighted = jnp.sum(jnp.where(matches, weights_in.astype(jnp.float32)[:, :, None], 0.0), axis=1)
    return (picks.astype(jnp.bfloat16), weighted.astype(jnp.bfloat16))


def dot(a, b, ca, cb):
    return lax.dot_general(a, b, (((ca,), (cb,)), ((), ())), preferred_element_type=jnp.float32)


def on_device(
    tokens,
    out_grad,
    route_ids,
    route_slots,
    route_weight,
    w_gate,
    w_up,
    w_down,
    proj_hidden,
    proj_grad,
    test_feats,
):
    experts = lax.axis_size("expert")
    groups = lax.axis_size("dp")
    halves = lax.axis_size("test")
    half = tokens.shape[1]
    slots = experts * CAP
    pick, weighted = pick_tables(route_ids, route_slots, route_weight, experts)
    in_buf = dot(pick, tokens, 0, 0).astype(jnp.bfloat16)
    grad_buf = dot(weighted, out_grad, 0, 0).astype(jnp.bfloat16)

    def exchange(rows):
        width = rows.shape[1]
        moved = lax.all_to_all(
            rows.reshape(experts, CAP, width), "expert", split_axis=0, concat_axis=0, tiled=True
        )
        return moved.reshape(slots, width)

    def spread(rows):
        full = lax.all_gather(rows, ("dp", "test"), axis=0, tiled=True)
        full = full.reshape(groups, halves, slots, half)
        return [full[:, h].reshape(groups * slots, half) for h in range(halves)]

    mine_in = exchange(in_buf)
    ins = spread(mine_in)
    mine_grad = exchange(grad_buf)
    grads = spread(mine_grad)

    gate_w, up_w, down_w = w_gate[0], w_up[0], w_down[0]

    def cut(arr, h, axis):
        return lax.slice_in_dim(arr, h * half, (h + 1) * half, axis=axis)

    gate_pre = sum(dot(ins[h], cut(gate_w, h, 0), 1, 0) for h in range(halves))
    up_pre = sum(dot(ins[h], cut(up_w, h, 0), 1, 0) for h in range(halves))
    sig = jax.nn.sigmoid(gate_pre)
    act = gate_pre * sig
    hidden = (act * up_pre).astype(jnp.bfloat16)
    proj_part = dot(hidden, proj_hidden[0], 1, 1)
    hid_grad = sum(dot(grads[h], cut(down_w, h, 1), 1, 1) for h in range(halves))
    up_grad = (hid_grad * act).astype(jnp.bfloat16)
    gate_grad = (hid_grad * up_pre * sig * (1.0 + gate_pre * (1.0 - sig))).astype(jnp.bfloat16)
    parts = [
        (dot(gate_grad, cut(gate_w, h, 0), 1, 1) + dot(up_grad, cut(up_w, h, 0), 1, 1)).astype(
            jnp.bfloat16
        )
        for h in range(halves)
    ]
    parts = jnp.stack([p.reshape(groups, slots, half) for p in parts], axis=1)
    mine_back = lax.psum_scatter(
        parts.reshape(groups * halves * slots, half), ("dp", "test"), scatter_dimension=0, tiled=True
    )
    back = exchange(mine_back.astype(jnp.bfloat16))
    in_grad = dot(pick, back, 1, 0).astype(jnp.bfloat16)

    hidden_vec = lax.psum(proj_part, ("dp", "test"))
    me = lax.axis_index("dp")
    hid_mine = lax.dynamic_slice_in_dim(hidden_vec, me * slots, slots, 0)
    grad_mine = sum(
        dot(lax.dynamic_slice_in_dim(grads[h], me * slots, slots, 0), cut(proj_grad[0], h, 1), 1, 1)
        for h in range(halves)
    )
    feature = (hid_mine[:, :, None] * grad_mine[:, None, :]).reshape(slots, -1).astype(jnp.bfloat16)
    score = dot(feature, test_feats[0], 1, 1).astype(jnp.bfloat16)
    scores = dot(pick, exchange(score), 1, 0)
    return (in_grad, scores)


def solution(mesh):
    placed = (
        P(("expert", "dp"), "test"),
        P(("expert", "dp"), "test"),
        P(("expert", "dp"), None),
        P(("expert", "dp"), None),
        P(("expert", "dp"), None),
        P("expert", None, ("dp", "test")),
        P("expert", None, ("dp", "test")),
        P("expert", ("dp", "test"), None),
        P("expert", None, ("dp", "test")),
        P("expert", None, None),
        P("expert", "test", None),
    )
    return jax.shard_map(
        on_device,
        mesh=mesh,
        in_specs=placed,
        out_specs=(P(("expert", "dp"), "test"), P(("expert", "dp"), "test")),
        check_vma=False,
    )
```

time: 660 us -> 317 us (0.48)
  waiting for transfers between devices: 480 us -> 151 us
  blocking collectives: 41.9 us -> 80.3 us
  matrix products: 49.1 us -> 19.2 us
  starting transfers between devices: 56.7 us -> 28.7 us
    all_to_all x4 -> x2, waiting for transfers between devices: 438 us -> 23.8 us  [exchange(): lax.all_to_all(rows.reshape(experts, CAP, width), 'expert', split_axis=0,...]
    all_to_all x0 -> x2, blocking collectives: none -> 80.3 us  [exchange(): lax.all_to_all(rows.reshape(experts, CAP, width), 'expert', split_axis=0,...]
    psum x1, waiting for transfers between devices: 0.02 us -> 64.8 us  [on_device(): hidden_vec = lax.psum(proj_part, ('dp', 'test'))]
    all_gather x5 -> x0, blocking collectives: 41.9 us -> none  [the longest x1 10.6 us: on_device(): lax.all_gather(tokens, 'test', axis=1, tiled=True)]
    dot_general x19 -> x18, matrix products: 49.1 us -> 19.2 us  [dot(): lax.dot_general(a, b, (((ca,), (cb,)), ((), ())), preferred_element_type=...]
    reduce_scatter x1, waiting for transfers between devices: 0.73 us -> 29.6 us  [on_device(): lax.psum_scatter(parts.reshape(groups * halves * slots, half), ('dp', 'te...]
    all_to_all x4 -> x2, starting transfers between devices: 56.3 us -> 28.5 us  [exchange(): lax.all_to_all(rows.reshape(experts, CAP, width), 'expert', split_axis=0,...]
    all_gather x2, waiting for transfers between devices: 41 us -> 33.2 us  [spread(): full = lax.all_gather(rows, ('dp', 'test'), axis=0, tiled=True)]
  transfers between devices with their start and end apart: 8 -> 6, of which waited for: 7 -> 4; matrix products, arithmetic and copies ran while one was open for 8% -> 6% of each run, Pallas kernels for 0% -> 0%
where the time goes in v1:
time: 317 us; the launch traced here: 312 us
  waiting for transfers between devices  151 us (48%)
  blocking collectives  80.3 us (25%)
  starting transfers between devices  28.7 us (9%)
  matrix products  19.2 us (6%)
  local copies, waits for them, and re-layouts  15 us (5%)
  between operations  14 us (4%)
  other arithmetic  3.41 us (1%)
    all_to_all x2, blocking collectives, exchange(): lax.all_to_all(rows.reshape(experts, CAP, width), 'expert', split_axis=0,...  80.3 us
    psum x1, waiting for transfers between devices, on_device(): hidden_vec = lax.psum(proj_part, ('dp', 'test'))  64.8 us
    all_gather x2, waiting for transfers between devices, spread(): full = lax.all_gather(rows, ('dp', 'test'), axis=0, tiled=True)  33.2 us
    reduce_scatter x1, waiting for transfers between devices, on_device(): lax.psum_scatter(parts.reshape(groups * halves * slots, half), ('dp', 'te...  29.6 us
    all_to_all x2, starting transfers between devices, exchange(): lax.all_to_all(rows.reshape(experts, CAP, width), 'expert', split_axis=0,...  28.5 us
    all_to_all x2, waiting for transfers between devices, exchange(): lax.all_to_all(rows.reshape(experts, CAP, width), 'expert', split_axis=0,...  23.8 us
    dot_general x18, matrix products, dot(): lax.dot_general(a, b, (((ca,), (cb,)), ((), ())), preferred_element_type=...  19.2 us
  transfers between devices with their start and end apart: 6, of which 4 were waited for; matrix products, arithmetic and copies ran while one was open for 6% of the time, Pallas kernels for 0%

profile of v1, /device:TPU:1, one launch (start us, length us, event | category | flops | bytes accessed | tf_op | source)
XLA Modules:
  0.0 311.9 jit_solution(14806735404021677156)
XLA Ops:
  7.2 0.8 add_select_fusion
  9.1 1.3 convolution_convert_fusion.1
  10.6 45.9 %all_to_all.20 = bf16[64,2,1792]{2,1,0:T(2,128)(2,1)S(1)} all-to-all(bf16[64,2,1792]{2,1,0:T(2,128)(2,1)S(1)} %reshape.58), channel_id=1, replica_groups=mesh['expert'=64,'dp'=4,'test'=2] {'expert'}, dimensions={0} | all-to-all | bytes 917504 | tf_op jit(solution)/shard_map/all_to_all | solution.py:47
  56.5 1.0 reshape.59
  58.1 34.4 %all_to_all.21 = bf16[64,2,1792]{2,1,0:T(2,128)(2,1)S(1)} all-to-all(bf16[64,2,1792]{2,1,0:T(2,128)(2,1)S(1)} %reshape.61), channel_id=1, replica_groups=mesh['expert'=64,'dp'=4,'test'=2] {'expert'}, dimensions={0} | all-to-all | bytes 917504 | tf_op jit(solution)/shard_map/all_to_all | solution.py:47
  92.4 0.9 reshape.62
  93.5 3.6 %fusion.41 = (bf16[4,1,128,1792]{3,2,1,0:T(8,128)(2,1)}, bf16[4,1,128,1792]{3,2,1,0:T(8,128)(2,1)S(1)}) fusion(bf16[4,2,128,1792]{3,2,1,0:T(8,128)(2,1)} %bitcast.73), kind=kLoop, calls=%fused_computation.61 | loop fusion | bytes 7340032 | tf_op jit(solution)/shard_map/slice | solution.py:55
  97.1 33.2 %all-gather.5.cloned.1.call-done = bf16[1024,1792]{1,0:T(8,128)(2,1)} async-done(((bf16[128,1792]{1,0:T(8,128)(2,1)}), bf16[1024,1792]{1,0:T(8,128)(2,1)}) %all-gather.5.cloned.1.call-update) | async-done | bytes 3670032 | tf_op jit(solution)/shard_map/all_gather | solution.py:53
  130.2 2.4 fusion.42
  138.0 2.4 fusion.4
  140.4 2.5 fusion.7
  142.9 0.9 fusion.30
  143.9 3.0 add_convert_fusion
  148.0 2.1 pad_maximum_fusion
  150.2 1.0 copy-done.6
  151.4 1.3 convolution_add_fusion.3
  152.8 64.8 %all-reduce.2.cloned.1.call-done = f32[512,64]{0,1:T(8,128)} async-done(((f32[512,64]{0,1:T(8,128)}), f32[512,64]{0,1:T(8,128)}) %all-reduce.2.cloned.1.call-update) | async-done | bytes 131088 | tf_op jit(solution)/shard_map/psum | solution.py:89
  218.6 1.1 convolution_convert_fusion.3
  219.7 14.5 %all-to-all-start.3 = ((bf16[64,2,128]{2,1,0:T(2,128)(2,1)}), bf16[64,2,128]{2,1,0:T(2,128)(2,1)S(1)}, u32[]{:S(2)}, u32[]{:S(2)}) async-start(bf16[64,2,128]{2,1,0:T(2,128)(2,1)} %bitcast.20), calls=%async_computation.4 | async-start | bytes 65536 | tf_op jit(solution)/shard_map/all_to_all | solution.py:47
  234.3 29.6 %reduce-scatter.2.cloned.1.call-done = bf16[128,1792]{1,0:T(8,128)(2,1)} async-done(((bf16[1024,1792]{1,0:T(8,128)(2,1)}), bf16[128,1792]{1,0:T(8,128)(2,1)}) %reduce-scatter.2.cloned.1.call-update) | async-done | bytes 458768 | tf_op jit(solution)/shard_map/reduce_scatter | solution.py:83
  263.8 2.0 reshape.65
  265.8 14.0 %all-to-all-start.2 = ((bf16[64,2,1792]{2,1,0:T(2,128)(2,1)}), bf16[64,2,1792]{2,1,0:T(2,128)(2,1)S(1)}, u32[]{:S(2)}, u32[]{:S(2)}) async-start(bf16[64,2,1792]{2,1,0:T(2,128)(2,1)} %reshape.65), calls=%async_computation.3 | async-start | bytes 917504 | tf_op jit(solution)/shard_map/all_to_all | solution.py:47
  280.5 23.8 %all-to-all-done.2 = bf16[64,2,1792]{2,1,0:T(2,128)(2,1)S(1)} async-done(((bf16[64,2,1792]{2,1,0:T(2,128)(2,1)}), bf16[64,2,1792]{2,1,0:T(2,128)(2,1)S(1)}, u32[]{:S(2)}, u32[]{:S(2)}) %all-to-all-start.2) | async-done | bytes 458784 | tf_op jit(solution)/shard_map/all_to_all | solution.py:47
  304.5 0.9 convolution_convert_fusion.2
  (47 shorter events, 10.7 us)
Async XLA Ops:
  7.2 211.4 %copy-start = (bf16[1,128,4096]{2,1,0:T(8,128)(2,1)S(1)}, bf16[1,128,4096]{2,1,0:T(8,128)(2,1)}, u32[]{:S(2)}) copy-start(bf16[1,128,4096]{2,1,0:T(8,128)(2,1)} %param.21) | copy-start | bytes 3145732
  7.2 86.3 %all-gather.3.cloned.1.call-start = ((), (), s32[]{:S(2)}) async-start(), calls=%async_computation.5 | async-start | bytes 4128768 | tf_op jit(solution)/shard_map/all_gather | solution.py:53
  9.1 48.5 %copy-start.8 = (bf16[64,1792]{1,0:T(8,128)(2,1)S(1)}, bf16[64,1792]{1,0:T(8,128)(2,1)}, u32[]{:S(2)}) copy-start(bf16[64,1792]{1,0:T(8,128)(2,1)} %param.11) | copy-start | bytes 688132
  57.5 72.7 %all-gather.5.cloned.1.call-start = ((), (), s32[]{:S(2)}) async-start(), calls=%async_computation.6 | async-start | bytes 4128768 | tf_op jit(solution)/shard_map/all_gather | solution.py:53
  93.4 124.2 %all-reduce.2.cloned.1.call-start = ((), (), s32[]{:S(2)}) async-start(), calls=%async_computation.8 | async-start | bytes 262144 | tf_op jit(solution)/shard_map/psum | solution.py:89
  130.2 2.4 copy-start.2
  132.6 1.2 copy-start.3
  135.1 1.2 copy-start.7
  135.8 1.6 copy-start.5
  140.4 2.5 copy-start.9
  143.8 120.0 %reduce-scatter.2.cloned.1.call-start = ((), (), s32[]{:S(2)}) async-start(), calls=%async_computation.7 | async-start | bytes 4128768 | tf_op jit(solution)/shard_map/reduce_scatter | solution.py:83
  143.9 3.3 %copy-start.1 = (f32[512,1792]{1,0:T(8,128)S(1)}, f32[512,1792]{1,0:T(8,128)}, u32[]{:S(2)}) copy-start(f32[512,1792]{1,0:T(8,128)} %fusion.7) | copy-start | bytes 11010052
  143.9 3.5 %copy-start.4 = (bf16[1,3584,128]{2,1,0:T(8,128)(2,1)S(1)}, bf16[1,3584,128]{2,1,0:T(8,128)(2,1)}, u32[]{:S(2)}) copy-start(bf16[1,3584,128]{2,1,0:T(8,128)(2,1)} %param.17) | copy-start | bytes 2752516
  150.1 1.0 copy-start.6
  219.7 46.1 %all-to-all-start.3 = ((bf16[64,2,128]{2,1,0:T(2,128)(2,1)}), bf16[64,2,128]{2,1,0:T(2,128)(2,1)S(1)}, u32[]{:S(2)}, u32[]{:S(2)}) async-start(bf16[64,2,128]{2,1,0:T(2,128)(2,1)} %bitcast.20), calls=%async_computation.4 | async-start | bytes 65536 | tf_op jit(solution)/shard_map/all_to_all | solution.py:47
  265.8 38.6 %all-to-all-start.2 = ((bf16[64,2,1792]{2,1,0:T(2,128)(2,1)}), bf16[64,2,1792]{2,1,0:T(2,128)(2,1)S(1)}, u32[]{:S(2)}, u32[]{:S(2)}) async-start(bf16[64,2,1792]{2,1,0:T(2,128)(2,1)} %reshape.65), calls=%async_computation.3 | async-start | bytes 917504 | tf_op jit(solution)/shard_map/all_to_all | solution.py:47
Sparse Core Ops, SparseCore 0:
  57.6 32.8 all-gather.2
  93.5 36.6 all-gather.4
  143.9 73.5 all-reduce.1
  220.3 43.5 reduce-scatter.1
